TPU v7x, 32 devices: a whole 2x2x4 slice. The times are simulated.
32 devices in a mesh: expert: 4 (over z), dp: 8 (over y, x, core).
Axes of the slice: x: 2, y: 2, z: 4, core: 2. Of those that a mesh axis runs over, the one named last changes fastest.
Arguments:
- tokens: bfloat16 [3072, 2304], P(('expert', 'dp')), may hold values from -6 to 6
- expert_ids: int32 [3072, 2], P(('expert', 'dp')), may hold values from 0 to 3, all different within a row; in each aligned block of 96 rows (0 to 95, 96 to 191, ...) at most 64 rows name the same one
- gate_weights: float32 [3072, 2], P(('expert', 'dp')), may hold values from 0.2 to 1
- request_lengths: int32 [32, 4], P(('expert', 'dp')), may hold values from 1 to 48, 96 in all within a row
- request_adapter: int32 [32, 4], P(('expert', 'dp')), may hold values from 0 to 63
- expert_weights: bfloat16 [4, 2, 2304, 5760], P('expert', None, None, 'dp'), may hold values from -0.125 to 0.125
- expert_down: bfloat16 [4, 5760, 2304], P('expert', 'dp'), may hold values from -0.078125 to 0.078125
- low_down: bfloat16 [4, 2304, 2048], P('expert', None, 'dp'), may hold values from -0.125 to 0.125
- low_up: bfloat16 [4, 2, 1024, 5760], P('expert', None, None, 'dp'), may hold values from -1.5 to 1.5
Outputs:
- mixed: bfloat16 [3072, 2304], P(('expert', 'dp'))
Inputs may be any that keep to these rules, and one draw needn't show every extreme that they name: `expert_ids`: each row names 2 different experts; within the rows of one device no expert is named by more than 64 rows, a bound that some block reaches. `request_lengths`: each row sums to 96, and its largest entry is exactly 48.
All inputs are finite; a program needn't handle non-finite values.
Results may differ from a plain program's by a relative error of at most 0.017.
Values may be sent and summed in bfloat16 or wider, within the bound.
No kernel may reach another device: no remote copies, remote signals or barrier semaphores. Data moves between devices by JAX's collectives and lax.ppermute only.
A program may use at most 192 MiB of HBM per device.

v0:
```python
import jax
import jax.numpy as jnp
from jax import lax
from jax.sharding import PartitionSpec as P

TOP = 2
RANK = 16


def body(
    tokens,
    expert_ids,
    gate_weights,
    request_lengths,
    request_adapter,
    expert_weights,
    expert_down,
    low_down,
    low_up,
):
    ways_expert = lax.axis_size("expert")
    local_tokens = tokens.shape[0]
    width = tokens.shape[1]
    experts_all = ways_expert * expert_down.shape[0]
    capacity = local_tokens * TOP * 4 // (3 * experts_all)
    slots_all = experts_all * capacity
    held = low_down.shape[2] // (2 * RANK)
    adapters_all = low_up.shape[2] // RANK
    values = tokens.astype(jnp.float32)
    normed = (values * lax.rsqrt(jnp.mean(values * values, axis=1, keepdims=True) + 1e-05)).astype(
        jnp.bfloat16
    )
    ends = jnp.cumsum(request_lengths[0])
    place = jnp.arange(local_tokens, dtype=jnp.int32)
    which = jnp.sum((place[:, None] >= ends[None, :]).astype(jnp.int32), axis=1)
    lookup = (
        which[:, None] == jnp.arange(request_lengths.shape[1], dtype=jnp.int32)[None, :]
    ).astype(jnp.int32)
    adapter = jnp.sum(lookup * request_adapter[0][None, :], axis=1)
    flat = expert_ids.reshape(-1)
    onehot = (flat[:, None] == jnp.arange(experts_all, dtype=jnp.int32)[None, :]).astype(jnp.int32)
    slot = jnp.sum((jnp.cumsum(onehot, axis=0) - onehot) * onehot, axis=1)
    target = flat * capacity + slot
    placement_weights = (jnp.arange(slots_all, dtype=jnp.int32)[:, None] == target[None, :]).astype(
        jnp.bfloat16
    )
    pairs = jnp.repeat(normed, TOP, axis=0)
    outgoing = (
        jnp.dot(placement_weights, pairs, preferred_element_type=jnp.float32)
        .astype(jnp.bfloat16)
        .reshape(experts_all, capacity, width)
    )
    pair_adapter = jnp.repeat(adapter, TOP).astype(jnp.float32)
    outgoing_ids = (
        jnp.dot(placement_weights.astype(jnp.float32), pair_adapter)
        .astype(jnp.bfloat16)
        .reshape(experts_all, capacity)
    )
    arrived, arrived_ids = (
        lax.all_to_all(outgoing, "expert", split_axis=0, concat_axis=0, tiled=True),
        lax.all_to_all(outgoing_ids, "expert", split_axis=0, concat_axis=0, tiled=True),
    )
    rows, labels_wire = (
        lax.all_gather(arrived.reshape(-1, width), "dp", axis=0, tiled=True),
        lax.all_gather(arrived_ids.reshape(-1), "dp", axis=0, tiled=True),
    )
    rows_total = rows.shape[0]
    labels = labels_wire.astype(jnp.int32)
    group = lax.axis_index("dp")
    projected = jnp.dot(rows, low_down[0], preferred_element_type=jnp.float32).reshape(
        rows_total, held, 2 * RANK
    )
    owned = (labels[:, None] == group * held + jnp.arange(held, dtype=jnp.int32)[None, :]).astype(
        jnp.float32
    )
    lowrank_part = jnp.sum(owned[:, :, None] * projected, axis=1)
    lowrank = lax.psum(lowrank_part.astype(jnp.bfloat16), "dp")
    marks = (labels[:, None] == jnp.arange(adapters_all, dtype=jnp.int32)[None, :]).astype(
        jnp.bfloat16
    )
    spread_gate = (marks[:, :, None] * lowrank[:, None, :RANK]).reshape(
        lax.axis_size("dp") * (ways_expert * capacity), adapters_all * RANK
    )
    sharded_up_weight = (marks[:, :, None] * lowrank[:, None, RANK:]).reshape(
        lax.axis_size("dp") * (ways_expert * capacity), adapters_all * RANK
    )
    gate = jnp.dot(rows, expert_weights[0, 0], preferred_element_type=jnp.float32) + jnp.dot(
        spread_gate, low_up[0, 0], preferred_element_type=jnp.float32
    )
    up = jnp.dot(rows, expert_weights[0, 1], preferred_element_type=jnp.float32) + jnp.dot(
        sharded_up_weight, low_up[0, 1], preferred_element_type=jnp.float32
    )
    hidden_activations = (jax.nn.silu(gate) * up).astype(jnp.bfloat16)
    mine = lax.psum_scatter(
        jnp.dot(hidden_activations, expert_down[0], preferred_element_type=jnp.float32).astype(
            jnp.bfloat16
        ),
        "dp",
        scatter_dimension=0,
        tiled=True,
    ).astype(jnp.float32)
    mine = mine.astype(jnp.bfloat16).reshape(ways_expert, capacity, width)
    back = lax.all_to_all(mine, "expert", split_axis=0, concat_axis=0, tiled=True)
    picked = jnp.dot(
        placement_weights.T, back.reshape(slots_all, width), preferred_element_type=jnp.float32
    ).reshape(local_tokens, TOP, width)
    mixed = values + jnp.sum(gate_weights[:, :, None] * picked, axis=1)
    return mixed.astype(jnp.bfloat16)


def solution(mesh):
    return jax.shard_map(
        body,
        mesh=mesh,
        in_specs=(
            P(("expert", "dp"), None),
            P(("expert", "dp"), None),
            P(("expert", "dp"), None),
            P(("expert", "dp"), None),
            P(("expert", "dp"), None),
            P("expert", None, None, "dp"),
            P("expert", "dp", None),
            P("expert", None, "dp"),
            P("expert", None, None, "dp"),
        ),
        out_specs=P(("expert", "dp"), None),
        check_vma=False,
    )
```

profile of v0, /device:TPU:0, one launch (start us, length us, event | category | flops | bytes accessed | tf_op | source)
XLA Modules:
  0.0 319.4 jit_solution(102362111478720045)
XLA Ops:
  6.5 0.0 copy-start
  6.5 0.0 all-gather.3.cloned.1.call-start
  6.5 0.9 copy.24
  7.5 0.1 reshape.192
  7.6 1.2 reduce-window.18
  8.9 0.1 slice.36
  8.9 0.1 copy.25
  9.1 0.1 copy.26
  9.2 0.1 add_bitcast_fusion
  9.3 1.2 fusion.24
  10.5 1.2 fusion.25
  11.7 0.0 copy-start.3
  11.7 0.0 copy-start.4
  11.7 1.4 broadcast_in_dim.4
  13.1 3.1 reshape.195
  16.2 1.6 convolution_convert_fusion.1
  17.9 34.8 %all_to_all.20 = bf16[4,64,2304]{2,1,0:T(8,128)(2,1)} all-to-all(bf16[4,64,2304]{2,1,0:T(8,128)(2,1)S(1)} %bitcast.58), channel_id=1, replica_groups=mesh['expert'=4,'dp'=8] {'expert'}, dimensions={0} | all-to-all | bytes 2359296 | tf_op jit(solution)/shard_map/all_to_all | solution.py:60
  52.6 0.0 all-gather.3.cloned.1.call-update
  52.7 0.0 copy-done.3
  52.7 0.2 reduce-window.20
  52.8 0.1 convert_reduce_fusion
  52.9 0.0 copy-done.4
  52.9 0.1 select_reduce_fusion
  53.0 0.1 broadcast_in_dim.5
  53.1 0.2 reshape.208
  53.3 0.2 fusion.28
  53.4 0.7 all_to_all.16
  54.1 3.2 %all-to-all-start.1 = ((bf16[4,1,64]{2,1,0:T(2,128)(2,1)}), bf16[4,1,64]{2,1,0:T(2,128)(2,1)S(1)}, u32[]{:S(2)}, u32[]{:S(2)}) async-start(bf16[4,1,64]{2,1,0:T(2,128)(2,1)} %all_to_all.16), calls=%async_computation.1 | async-start | bytes 4096 | tf_op jit(solution)/shard_map/all_to_all | solution.py:61
  57.4 0.0 all-reduce.3.cloned.1.call-start
  57.4 2.4 copy.28
  59.9 2.9 all-to-all-done.1
  62.8 0.1 reshape.204
  62.9 8.9 %all-gather = bf16[8,1,256]{2,1,0:T(2,128)(2,1)S(1)} all-gather(bf16[1,1,256]{2,1,0:T(2,128)(2,1)S(1)} %reshape.204), channel_id=1, replica_groups=mesh['expert'=4,'dp'=8] {'dp'}, dimensions={0}, use_global_device_ids=true | all-gather | bytes 4608 | tf_op jit(solution)/shard_map/all_gather | solution.py:65
  71.8 0.1 compare_convert_fusion
  71.9 0.8 fusion.27
  72.6 38.1 %all-gather.3.cloned.1.call-done = bf16[2048,2304]{1,0:T(8,128)(2,1)} async-done(((bf16[256,2304]{1,0:T(8,128)(2,1)}), bf16[2048,2304]{1,0:T(8,128)(2,1)}) %all-gather.3.cloned.1.call-update) | async-done | bytes 9437200 | tf_op jit(solution)/shard_map/all_gather | solution.py:64
  110.8 7.3 %fusion.21 = bf16[2048,32]{0,1:T(8,128)(2,1)} fusion(bf16[8,32,2304]{2,1,0:T(8,128)(2,1)} %bitcast.62, bf16[2048,2304]{1,0:T(8,128)(2,1)} %all-gather.3.cloned.1.call-done, f32[2048,8]{0,1:T(8,128)S(1)} %compare_convert_fusion), kind=kOutput, calls=%fused_computation.23 | convolution fusion | flops 2416902144 | bytes 10813440 | tf_op jit(solution)/shard_map/dot_general | solution.py:70
  118.0 0.0 all-reduce.3.cloned.1.call-update
  118.1 0.2 reduce-scatter.2.cloned.1.call-start
  118.3 12.2 %fusion.3 = f32[2048,720]{0,1:T(8,128)} fusion(bf16[2048,2304]{1,0:T(8,128)(2,1)} %all-gather.3.cloned.1.call-done, bf16[1,2,2304,720]{2,3,1,0:T(8,128)(2,1)} %param.14), kind=kOutput, calls=%fused_computation.7 | convolution fusion | flops 6794772480 | bytes 18653184 | tf_op jit(solution)/shard_map/dot_general | solution.py:90
  130.5 12.2 %fusion.5 = f32[2048,720]{0,1:T(8,128)} fusion(bf16[2048,2304]{1,0:T(8,128)(2,1)} %all-gather.3.cloned.1.call-done, bf16[1,2,2304,720]{2,3,1,0:T(8,128)(2,1)} %param.14), kind=kOutput, calls=%fused_computation.9 | convolution fusion | flops 6794772480 | bytes 18653184 | tf_op jit(solution)/shard_map/dot_general | solution.py:87
  142.8 28.4 %all-reduce.3.cloned.1.call-done = bf16[2048,32]{0,1:T(8,128)(2,1)} async-done(((bf16[2048,32]{0,1:T(8,128)(2,1)}), bf16[2048,32]{0,1:T(8,128)(2,1)}) %all-reduce.3.cloned.1.call-update) | async-done | bytes 131088 | tf_op jit(solution)/shard_map/psum | solution.py:77
  171.2 0.9 fusion.35
  172.1 0.0 copy-start.2
  172.1 3.7 %broadcast_multiply_fusion = (bf16[2048,64,16]{0,2,1:T(8,128)(2,1)}, bf16[2048,64,16]{0,2,1:T(8,128)(2,1)S(1)}) fusion(bf16[2048,16]{0,1:T(8,128)(2,1)S(1)} %get-tuple-element.7, bf16[2048,64]{0,1:T(8,128)(2,1)} %fusion.27, bf16[2048,16]{0,1:T(8,128)(2,1)S(1)} %get-tuple-element.8), kind=kLoop, calls=%fused_computation.15 | loop fusion | flops 4194304 | bytes 8781824 | tf_op jit(solution)/shard_map/mul | solution.py:84
  175.8 0.0 copy-done.2
  175.8 5.2 %fusion.15 = f32[2048,720]{0,1:T(8,128)} fusion(bf16[2048,1024]{0,1:T(8,128)(2,1)S(1)} %bitcast.61, bf16[1,2,1024,720]{2,3,1,0:T(8,128)(2,1)S(1)} %copy-done.2), kind=kOutput, calls=%fused_computation.18 | convolution fusion | flops 3019898880 | bytes 11567104 | tf_op jit(solution)/shard_map/dot_general | solution.py:87
  181.0 0.0 copy-done
  181.0 18.9 %convolution_convert_fusion = bf16[2048,2304]{1,0:T(8,128)(2,1)} fusion(bf16[1,720,2304]{2,1,0:T(8,128)(2,1)S(1)} %copy-done, f32[2048,720]{0,1:T(8,128)} %fusion.3, f32[2048,720]{0,1:T(8,128)} %fusion.5, f32[2048,720]{0,1:T(8,128)} %fusion.15, bf16[2048,1024]{0,1:T(8,128)(2,1)} %bitcast.60, bf16[1,2,1024,720]{2,3,1,0:T(8,128)(2,1)} %param.17), kind=kOutput, calls=%fused_computation | convolution fusion | flops 9831186432 | bytes 36118528 | tf_op jit(solution)/shard_map/dot_general | solution.py:95
  199.9 0.0 copy-start.1
  199.9 0.0 reduce-scatter.2.cloned.1.call-update
  199.9 76.0 %reduce-scatter.2.cloned.1.call-done = bf16[256,2304]{1,0:T(8,128)(2,1)} async-done(((bf16[2048,2304]{1,0:T(8,128)(2,1)}), bf16[256,2304]{1,0:T(8,128)(2,1)}) %reduce-scatter.2.cloned.1.call-update) | async-done | bytes 1179664 | tf_op jit(solution)/shard_map/reduce_scatter | solution.py:94
  276.0 4.6 %all-to-all-start.2 = ((bf16[4,64,2304]{2,1,0:T(8,128)(2,1)}), bf16[4,64,2304]{2,1,0:T(8,128)(2,1)}, u32[]{:S(2)}, u32[]{:S(2)}) async-start(bf16[4,64,2304]{2,1,0:T(8,128)(2,1)} %bitcast.63), calls=%async_computation.3 | async-start | bytes 2359296 | tf_op jit(solution)/shard_map/all_to_all | solution.py:103
  280.6 0.1 iota_compare_fusion.4
  280.7 0.1 eq.104
  280.7 28.5 %all-to-all-done.2 = bf16[4,64,2304]{2,1,0:T(8,128)(2,1)} async-done(((bf16[4,64,2304]{2,1,0:T(8,128)(2,1)}), bf16[4,64,2304]{2,1,0:T(8,128)(2,1)}, u32[]{:S(2)}, u32[]{:S(2)}) %all-to-all-start.2) | async-done | bytes 1179680 | tf_op jit(solution)/shard_map/all_to_all | solution.py:103
  309.2 0.0 copy-done.1
  309.2 1.7 fusion.20
  311.0 1.9 fusion.26
  (14 shorter events, 0.2 us)
Async XLA Ops:
  6.5 174.4 %copy-start = (bf16[1,720,2304]{2,1,0:T(8,128)(2,1)S(1)}, bf16[1,720,2304]{2,1,0:T(8,128)(2,1)}, u32[]{:S(2)}) copy-start(bf16[1,720,2304]{2,1,0:T(8,128)(2,1)} %param.15) | copy-start | bytes 9953284
  6.5 104.2 %all-gather.3.cloned.1.call-start = ((), (), s32[]{:S(2)}) async-start(), calls=%async_computation.4 | async-start | bytes 10616832 | tf_op jit(solution)/shard_map/all_gather | solution.py:64
  11.7 41.0 %copy-start.3 = (s32[1,4]{1,0:T(1,128)S(1)}, s32[1,4]{1,0:T(1,128)}, u32[]{:S(2)}) copy-start(s32[1,4]{1,0:T(1,128)} %param.12) | copy-start | bytes 52
  11.7 41.2 %copy-start.4 = (s32[1,4]{1,0:T(1,128)S(1)}, s32[1,4]{1,0:T(1,128)}, u32[]{:S(2)}) copy-start(s32[1,4]{1,0:T(1,128)} %param.13) | copy-start | bytes 52
  54.1 8.7 %all-to-all-start.1 = ((bf16[4,1,64]{2,1,0:T(2,128)(2,1)}), bf16[4,1,64]{2,1,0:T(2,128)(2,1)S(1)}, u32[]{:S(2)}, u32[]{:S(2)}) async-start(bf16[4,1,64]{2,1,0:T(2,128)(2,1)} %all_to_all.16), calls=%async_computation.1 | async-start | bytes 4096 | tf_op jit(solution)/shard_map/all_to_all | solution.py:61
  57.4 113.8 %all-reduce.3.cloned.1.call-start = ((), (), s32[]{:S(2)}) async-start(), calls=%async_computation.5 | async-start | bytes 262144 | tf_op jit(solution)/shard_map/psum | solution.py:77
  118.1 157.9 %reduce-scatter.2.cloned.1.call-start = ((), (), s32[]{:S(2)}) async-start(), calls=%async_computation.6 | async-start | bytes 10616832 | tf_op jit(solution)/shard_map/reduce_scatter | solution.py:94
  172.1 3.7 %copy-start.2 = (bf16[1,2,1024,720]{2,3,1,0:T(8,128)(2,1)S(1)}, bf16[1,2,1024,720]{2,3,1,0:T(8,128)(2,1)}, u32[]{:S(2)}) copy-start(bf16[1,2,1024,720]{2,3,1,0:T(8,128)(2,1)} %param.17) | copy-start | bytes 8847364
  199.9 109.3 %copy-start.1 = (f32[96,2]{0,1:T(2,128)S(1)}, f32[96,2]{0,1:T(2,128)}, u32[]{:S(2)}) copy-start(f32[96,2]{0,1:T(2,128)} %param.11) | copy-start | bytes 2308
  276.0 33.2 %all-to-all-start.2 = ((bf16[4,64,2304]{2,1,0:T(8,128)(2,1)}), bf16[4,64,2304]{2,1,0:T(8,128)(2,1)}, u32[]{:S(2)}, u32[]{:S(2)}) async-start(bf16[4,64,2304]{2,1,0:T(8,128)(2,1)} %bitcast.63), calls=%async_computation.3 | async-start | bytes 2359296 | tf_op jit(solution)/shard_map/all_to_all | solution.py:103
Sparse Core Ops, SparseCore 0:
  52.8 57.9 all-gather.2
  118.2 52.9 all-reduce.2
  200.1 75.8 reduce-scatter.1
where the time goes:
time: 320 us; the launch traced here: 319 us
  waiting for transfers between devices  174 us (54%)
  matrix products  59.4 us (19%)
  blocking collectives  43.7 us (14%)
  between operations  13.3 us (4%)
  other arithmetic  10.7 us (3%)
  local copies, waits for them, and re-layouts  10.3 us (3%)
  starting transfers between devices  8.09 us (3%)
    reduce_scatter x1, waiting for transfers between devices, body(): lax.psum_scatter(jnp.dot(hidden_activations, expert_down[0], preferred_el...  76 us
    all_gather x1, waiting for transfers between devices, body(): lax.all_gather(arrived.reshape(-1, width), 'dp', axis=0, tiled=True)  38.1 us
    all_to_all x1, blocking collectives, body(): lax.all_to_all(outgoing, 'expert', split_axis=0, concat_axis=0, tiled=True)  34.8 us
    all_to_all x1, waiting for transfers between devices, body(): lax.all_to_all(mine, 'expert', split_axis=0, concat_axis=0, tiled=True)  28.5 us
    psum x1, waiting for transfers between devices, body(): lowrank = lax.psum(lowrank_part.astype(jnp.bfloat16), 'dp')  28.4 us
    dot_general x1, matrix products, body(): jnp.dot(hidden_activations, expert_down[0], preferred_element_type=jnp.fl...  18.9 us
    dot_general x1, matrix products, body(): jnp.dot(rows, expert_weights[0, 0], preferred_element_type=jnp.float32)  12.2 us
    dot_general x1, matrix products, body(): jnp.dot(rows, expert_weights[0, 1], preferred_element_type=jnp.float32)  12.2 us
  transfers between devices with their start and end apart: 5, of which 5 were waited for; matrix products, arithmetic and copies ran while one was open for 9% of the time, Pallas kernels for 0%

commit v1 on v0

--- a/solution.py
+++ b/solution.py
@@ -74,7 +74,7 @@
         jnp.float32
     )
     lowrank_part = jnp.sum(owned[:, :, None] * projected, axis=1)
-    lowrank = lax.psum(lowrank_part.astype(jnp.bfloat16), "dp")
+    lowrank = jnp.sum(lax.all_gather(lowrank_part.astype(jnp.bfloat16), "dp"), axis=0)
     marks = (labels[:, None] == jnp.arange(adapters_all, dtype=jnp.int32)[None, :]).astype(
         jnp.bfloat16
     )

time: 320 us -> 294 us (0.919)
  waiting for transfers between devices: 174 us -> 146 us
    psum x1 -> x0, waiting for transfers between devices: 28.4 us -> none  [body(): lowrank = lax.psum(lowrank_part.astype(jnp.bfloat16), 'dp')]
  transfers between devices with their start and end apart: 5 -> 5, of which waited for: 5 -> 4; matrix products, arithmetic and copies ran while one was open for 9% -> 10% of each run, Pallas kernels for 0% -> 0%
where the time goes in v1:
time: 294 us; the launch traced here: 293 us
  waiting for transfers between devices  146 us (50%)
  matrix products  59.6 us (20%)
  blocking collectives  43.7 us (15%)
  between operations  13.3 us (5%)
  other arithmetic  11.4 us (4%)
  local copies, waits for them, and re-layouts  11.2 us (4%)
  starting transfers between devices  8.06 us (3%)
    reduce_scatter x1, waiting for transfers between devices, body(): lax.psum_scatter(jnp.dot(hidden_activations, expert_down[0], preferred_el...  76.7 us
    all_gather x1, waiting for transfers between devices, body(): lax.all_gather(arrived.reshape(-1, width), 'dp', axis=0, tiled=True)  38.1 us
    all_to_all x1, blocking collectives, body(): lax.all_to_all(outgoing, 'expert', split_axis=0, concat_axis=0, tiled=True)  34.8 us
    all_to_all x1, waiting for transfers between devices, body(): lax.all_to_all(mine, 'expert', split_axis=0, concat_axis=0, tiled=True)  28.5 us
    dot_general x1, matrix products, body(): jnp.dot(hidden_activations, expert_down[0], preferred_element_type=jnp.fl...  19.2 us
    dot_general x1, matrix products, body(): jnp.dot(rows, expert_weights[0, 0], preferred_element_type=jnp.float32)  12.2 us
    dot_general x1, matrix products, body(): jnp.dot(rows, expert_weights[0, 1], preferred_element_type=jnp.float32)  12.2 us
    all_gather x1, blocking collectives, body(): lax.all_gather(arrived_ids.reshape(-1), 'dp', axis=0, tiled=True)  8.9 us
  transfers between devices with their start and end apart: 5, of which 4 were waited for; matrix products, arithmetic and copies ran while one was open for 10% of the time, Pallas kernels for 0%

profile of v1, /device:TPU:0, one launch (start us, length us, event | category | flops | bytes accessed | tf_op | source)
XLA Modules:
  0.0 293.5 jit_solution(11929419180505860142)
XLA Ops:
  6.5 0.0 copy-start
  6.5 0.0 all-gather.5.cloned.1.call-start
  6.5 0.9 copy.24
  7.5 0.1 reshape.200
  7.6 1.2 reduce-window.18
  8.9 0.1 slice.36
  8.9 0.1 copy.25
  9.1 0.1 copy.26
  9.2 0.1 add_bitcast_fusion
  9.3 1.2 fusion.24
  10.5 1.2 fusion.25
  11.7 0.0 copy-start.3
  11.7 0.0 copy-start.4
  11.7 1.4 broadcast_in_dim.4
  13.1 3.1 %reshape.203 = bf16[192,2304]{1,0:T(8,128)(2,1)} reshape(bf16[96,2,2304]{2,1,0:T(2,128)(2,1)} %broadcast_in_dim.4) | data formatting | bytes 1769472 | tf_op jit(solution)/shard_map/reshape | solution.py:47
  16.2 1.6 convolution_convert_fusion.1
  17.9 34.8 %all_to_all.20 = bf16[4,64,2304]{2,1,0:T(8,128)(2,1)} all-to-all(bf16[4,64,2304]{2,1,0:T(8,128)(2,1)S(1)} %bitcast.63), channel_id=1, replica_groups=mesh['expert'=4,'dp'=8] {'expert'}, dimensions={0} | all-to-all | bytes 2359296 | tf_op jit(solution)/shard_map/all_to_all | solution.py:60
  52.6 0.0 all-gather.5.cloned.1.call-update
  52.7 0.0 copy-done.3
  52.7 0.2 reduce-window.20
  52.8 0.1 convert_reduce_fusion
  52.9 0.0 copy-done.4
  52.9 0.1 select_reduce_fusion
  53.0 0.1 broadcast_in_dim.5
  53.1 0.2 reshape.217
  53.3 0.2 fusion.28
  53.4 0.7 all_to_all.16
  54.1 3.2 %all-to-all-start.1 = ((bf16[4,1,64]{2,1,0:T(2,128)(2,1)}), bf16[4,1,64]{2,1,0:T(2,128)(2,1)S(1)}, u32[]{:S(2)}, u32[]{:S(2)}) async-start(bf16[4,1,64]{2,1,0:T(2,128)(2,1)} %all_to_all.16), calls=%async_computation.1 | async-start | bytes 4096 | tf_op jit(solution)/shard_map/all_to_all | solution.py:61
  57.4 0.0 all-gather.7.cloned.1.call-start
  57.4 2.4 copy.28
  59.9 2.9 all-to-all-done.1
  62.8 0.1 reshape.213
  62.9 8.9 %all-gather.1 = bf16[8,1,256]{2,1,0:T(2,128)(2,1)S(1)} all-gather(bf16[1,1,256]{2,1,0:T(2,128)(2,1)S(1)} %reshape.213), channel_id=1, replica_groups=mesh['expert'=4,'dp'=8] {'dp'}, dimensions={0}, use_global_device_ids=true | all-gather | bytes 4608 | tf_op jit(solution)/shard_map/all_gather | solution.py:65
  71.8 0.1 compare_convert_fusion
  71.9 0.8 fusion.27
  72.6 38.1 %all-gather.5.cloned.1.call-done = bf16[2048,2304]{1,0:T(8,128)(2,1)} async-done(((bf16[256,2304]{1,0:T(8,128)(2,1)}), bf16[2048,2304]{1,0:T(8,128)(2,1)}) %all-gather.5.cloned.1.call-update) | async-done | bytes 9437200 | tf_op jit(solution)/shard_map/all_gather | solution.py:64
  110.8 7.3 %fusion.21 = bf16[2048,32]{0,1:T(8,128)(2,1)} fusion(bf16[8,32,2304]{2,1,0:T(8,128)(2,1)} %bitcast.67, bf16[2048,2304]{1,0:T(8,128)(2,1)} %all-gather.5.cloned.1.call-done, f32[2048,8]{0,1:T(8,128)S(1)} %compare_convert_fusion), kind=kOutput, calls=%fused_computation.23 | convolution fusion | flops 2416902144 | bytes 10813440 | tf_op jit(solution)/shard_map/dot_general | solution.py:70
  118.1 0.0 all-gather.7.cloned.1.call-update
  118.1 0.2 reduce-scatter.2.cloned.1.call-start
  118.3 12.2 %fusion.3 = f32[2048,720]{0,1:T(8,128)} fusion(bf16[2048,2304]{1,0:T(8,128)(2,1)} %all-gather.5.cloned.1.call-done, bf16[1,2,2304,720]{2,3,1,0:T(8,128)(2,1)} %param.14), kind=kOutput, calls=%fused_computation.7 | convolution fusion | flops 6794772480 | bytes 18653184 | tf_op jit(solution)/shard_map/dot_general | solution.py:90
  130.5 12.2 %fusion.5 = f32[2048,720]{0,1:T(8,128)} fusion(bf16[2048,2304]{1,0:T(8,128)(2,1)} %all-gather.5.cloned.1.call-done, bf16[1,2,2304,720]{2,3,1,0:T(8,128)(2,1)} %param.14), kind=kOutput, calls=%fused_computation.9 | convolution fusion | flops 6794772480 | bytes 18653184 | tf_op jit(solution)/shard_map/dot_general | solution.py:87
  142.7 0.0 all-gather.7.cloned.1.call-done
  142.7 1.8 copy.31
  144.6 0.8 bitcast_reduce_fusion
  145.4 0.0 copy-start.2
  145.4 3.7 %broadcast_multiply_fusion = (bf16[2048,64,16]{0,2,1:T(8,128)(2,1)}, bf16[2048,64,16]{0,2,1:T(8,128)(2,1)S(1)}) fusion(bf16[2048,16]{0,1:T(8,128)(2,1)S(1)} %get-tuple-element.7, bf16[2048,64]{0,1:T(8,128)(2,1)} %fusion.27, bf16[2048,16]{0,1:T(8,128)(2,1)S(1)} %get-tuple-element.8), kind=kLoop, calls=%fused_computation.15 | loop fusion | flops 4194304 | bytes 8781824 | tf_op jit(solution)/shard_map/mul | solution.py:84
  149.1 0.0 copy-done.2
  149.1 5.2 %fusion.15 = f32[2048,720]{0,1:T(8,128)} fusion(bf16[2048,1024]{0,1:T(8,128)(2,1)S(1)} %bitcast.66, bf16[1,2,1024,720]{2,3,1,0:T(8,128)(2,1)S(1)} %copy-done.2), kind=kOutput, calls=%fused_computation.18 | convolution fusion | flops 3019898880 | bytes 11567104 | tf_op jit(solution)/shard_map/dot_general | solution.py:87
  154.3 0.0 copy-done
  154.3 19.2 %convolution_convert_fusion = bf16[2048,2304]{1,0:T(8,128)(2,1)} fusion(bf16[1,720,2304]{2,1,0:T(8,128)(2,1)S(1)} %copy-done, f32[2048,720]{0,1:T(8,128)} %fusion.3, f32[2048,720]{0,1:T(8,128)} %fusion.5, f32[2048,720]{0,1:T(8,128)} %fusion.15, bf16[2048,1024]{0,1:T(8,128)(2,1)} %bitcast.65, bf16[1,2,1024,720]{2,3,1,0:T(8,128)(2,1)} %param.17), kind=kOutput, calls=%fused_computation | convolution fusion | flops 9831186432 | bytes 36118528 | tf_op jit(solution)/shard_map/dot_general | solution.py:95
  173.4 0.0 copy-start.1
  173.4 0.0 reduce-scatter.2.cloned.1.call-update
  173.4 76.7 %reduce-scatter.2.cloned.1.call-done = bf16[256,2304]{1,0:T(8,128)(2,1)} async-done(((bf16[2048,2304]{1,0:T(8,128)(2,1)}), bf16[256,2304]{1,0:T(8,128)(2,1)}) %reduce-scatter.2.cloned.1.call-update) | async-done | bytes 1179664 | tf_op jit(solution)/shard_map/reduce_scatter | solution.py:94
  250.1 4.6 %all-to-all-start.2 = ((bf16[4,64,2304]{2,1,0:T(8,128)(2,1)}), bf16[4,64,2304]{2,1,0:T(8,128)(2,1)}, u32[]{:S(2)}, u32[]{:S(2)}) async-start(bf16[4,64,2304]{2,1,0:T(8,128)(2,1)} %bitcast.68), calls=%async_computation.3 | async-start | bytes 2359296 | tf_op jit(solution)/shard_map/all_to_all | solution.py:103
  254.7 0.1 iota_compare_fusion.4
  254.8 0.1 eq.104
  254.8 28.5 %all-to-all-done.2 = bf16[4,64,2304]{2,1,0:T(8,128)(2,1)} async-done(((bf16[4,64,2304]{2,1,0:T(8,128)(2,1)}), bf16[4,64,2304]{2,1,0:T(8,128)(2,1)}, u32[]{:S(2)}, u32[]{:S(2)}) %all-to-all-start.2) | async-done | bytes 1179680 | tf_op jit(solution)/shard_map/all_to_all | solution.py:103
  283.3 0.0 copy-done.1
  283.3 1.7 fusion.20
  285.1 1.9 fusion.26
  (15 shorter events, 0.2 us)
Async XLA Ops:
  6.5 147.7 %copy-start = (bf16[1,720,2304]{2,1,0:T(8,128)(2,1)S(1)}, bf16[1,720,2304]{2,1,0:T(8,128)(2,1)}, u32[]{:S(2)}) copy-start(bf16[1,720,2304]{2,1,0:T(8,128)(2,1)} %param.15) | copy-start | bytes 9953284
  6.5 104.2 %all-gather.5.cloned.1.call-start = ((), (), s32[]{:S(2)}) async-start(), calls=%async_computation.4 | async-start | bytes 10616832 | tf_op jit(solution)/shard_map/all_gather | solution.py:64
  11.7 41.0 %copy-start.3 = (s32[1,4]{1,0:T(1,128)S(1)}, s32[1,4]{1,0:T(1,128)}, u32[]{:S(2)}) copy-start(s32[1,4]{1,0:T(1,128)} %param.12) | copy-start | bytes 52
  11.7 41.2 %copy-start.4 = (s32[1,4]{1,0:T(1,128)S(1)}, s32[1,4]{1,0:T(1,128)}, u32[]{:S(2)}) copy-start(s32[1,4]{1,0:T(1,128)} %param.13) | copy-start | bytes 52
  54.1 8.7 %all-to-all-start.1 = ((bf16[4,1,64]{2,1,0:T(2,128)(2,1)}), bf16[4,1,64]{2,1,0:T(2,128)(2,1)S(1)}, u32[]{:S(2)}, u32[]{:S(2)}) async-start(bf16[4,1,64]{2,1,0:T(2,128)(2,1)} %all_to_all.16), calls=%async_computation.1 | async-start | bytes 4096 | tf_op jit(solution)/shard_map/all_to_all | solution.py:61
  57.4 85.4 %all-gather.7.cloned.1.call-start = ((), (), s32[]{:S(2)}) async-start(), calls=%async_computation.6 | async-start | bytes 1179648 | tf_op jit(solution)/shard_map/all_gather | solution.py:77
  118.1 132.0 %reduce-scatter.2.cloned.1.call-start = ((), (), s32[]{:S(2)}) async-start(), calls=%async_computation.5 | async-start | bytes 10616832 | tf_op jit(solution)/shard_map/reduce_scatter | solution.py:94
  145.4 3.7 %copy-start.2 = (bf16[1,2,1024,720]{2,3,1,0:T(8,128)(2,1)S(1)}, bf16[1,2,1024,720]{2,3,1,0:T(8,128)(2,1)}, u32[]{:S(2)}) copy-start(bf16[1,2,1024,720]{2,3,1,0:T(8,128)(2,1)} %param.17) | copy-start | bytes 8847364
  173.4 109.9 %copy-start.1 = (f32[96,2]{0,1:T(2,128)S(1)}, f32[96,2]{0,1:T(2,128)}, u32[]{:S(2)}) copy-start(f32[96,2]{0,1:T(2,128)} %param.11) | copy-start | bytes 2308
  250.1 33.2 %all-to-all-start.2 = ((bf16[4,64,2304]{2,1,0:T(8,128)(2,1)}), bf16[4,64,2304]{2,1,0:T(8,128)(2,1)}, u32[]{:S(2)}, u32[]{:S(2)}) async-start(bf16[4,64,2304]{2,1,0:T(8,128)(2,1)} %bitcast.68), calls=%async_computation.3 | async-start | bytes 2359296 | tf_op jit(solution)/shard_map/all_to_all | solution.py:103
Sparse Core Ops, SparseCore 0:
  52.8 57.9 all-gather.4
  118.2 23.4 all-gather.6
  173.6 76.4 reduce-scatter.1
